TPU v7x, 256 devices: a whole 4x4x8 slice. The times are simulated.
256 devices in a mesh: ctx: 64 (over z, x, core), head: 4 (over y).
Axes of the slice: x: 4, y: 4, z: 8, core: 2. Of those that a mesh axis runs over, the one named last changes fastest.
Arguments:
- mixer_input: bfloat16 [2, 4096, 16384], P(None, ('ctx', 'head')), may hold values from -6 to 6
- gate_input: bfloat16 [2, 4096, 16384], P(None, ('ctx', 'head')), may hold values from -6 to 6
- step_input: bfloat16 [2, 4096, 16384], P(None, ('ctx', 'head'))
- state_proj: bfloat16 [2, 4096, 32], P(None, 'ctx'), may hold values from -4 to 4
- conv_weight: bfloat16 [4, 16384], replicated, may hold values from -3 to 3
- conv_bias: float32 [16384], replicated, may hold values from -1 to 1
- step_bias: float32 [16384], P('head')
- decay_log: float32 [16, 16384], P(None, 'head'), may hold values from -0.7 to 0.7
- skip_gain: float32 [16384], P('head'), may hold values from 0.5 to 1.5
- query_states: bfloat16 [2, 4096, 8192], P(None, ('ctx', 'head')), may hold values from -5 to 5
- key_states: bfloat16 [2, 4096, 1024], P(None, ('ctx', 'head')), may hold values from -5 to 5
- value_states: bfloat16 [2, 4096, 1024], P(None, ('ctx', 'head')), may hold values from -6 to 6
- lengths: int32 [2], replicated, may hold values from 1024 to 4096, as said below
Outputs:
- mixer_output: bfloat16 [2, 4096, 16384], P(None, 'ctx', 'head')
- attention_output: bfloat16 [2, 4096, 8192], P(None, 'ctx', 'head')
Inputs may be any that keep to these rules, and one draw needn't show every extreme that they name: `lengths`: one of the 2 sequences has length 4096.
All inputs are finite; a program needn't handle non-finite values.
Results may differ from a plain program's by a relative error of at most 0.0043.
Values may be sent and summed in bfloat16 or wider, within the bound.
No kernel may reach another device: no remote copies, remote signals or barrier semaphores. Data moves between devices by JAX's collectives and lax.ppermute only.
A program may use at most 256 MiB of HBM per device.

v0:
```python
import math
import jax
import jax.numpy as jnp
from jax import lax
from jax.sharding import PartitionSpec as P

HD = 128
neg_large = -1e30


def passed_along(block, axis, distance):
    devices = range(lax.axis_size(axis))
    route = [(i - distance, i) for i in devices if i - distance in devices]
    return lax.ppermute(block, axis, route)


def carried_in(value, axis, join, neutral):
    count, mine = (lax.axis_size(axis), lax.axis_index(axis))
    pieces = jax.tree.map(lambda part: lax.all_gather(part, axis), value)
    total = jax.tree.map(
        lambda part, zero: jnp.full_like(part, 0) + jnp.asarray(zero, part.dtype), value, neutral
    )

    def step(position, total):
        longer = join(total, jax.tree.map(lambda part: part[position], pieces))
        return jax.tree.map(lambda new, old: jnp.where(position < mine, new, old), longer, total)

    return lax.fori_loop(0, count - 1, step, total)


def conv_rows(padded, conv_weight, conv_bias, row_count):
    running = (
        jnp.zeros((padded.shape[0], row_count, padded.shape[2]), jnp.float32)
        + conv_bias[None, None, :]
    )
    for tap_index in range(conv_weight.shape[0]):
        window = padded[:, tap_index : tap_index + row_count, :].astype(jnp.float32)
        running = running + window * conv_weight[tap_index].astype(jnp.float32)[None, None, :]
    return jax.nn.silu(running).astype(jnp.bfloat16)


def block_width(key_count):
    chosen = min(key_count, 512)
    while key_count % chosen != 0:
        chosen = chosen - 1
    return chosen


def empty_state(query_block):
    state_shape = (
        query_block.shape[0],
        query_block.shape[2],
        query_block.shape[3],
        query_block.shape[1],
    )
    return (
        jnp.full(state_shape, neg_large, jnp.float32),
        jnp.zeros(state_shape, jnp.float32),
        jnp.zeros(state_shape + (query_block.shape[4],), jnp.float32),
    )


def attend_block(
    carried, query_block, query_offset, key_block, value_block, key_offset, logit_scale_factor
):
    query_count = query_block.shape[1]
    key_count = key_block.shape[1]

    def compute(previous):
        row_peak, softmax_divisor, accumulated = previous
        score_matrix = (
            jnp.einsum(
                "brkgd,bskd->bkgrs", query_block, key_block, preferred_element_type=jnp.float32
            )
            * logit_scale_factor
        )
        query_pos = query_offset + jnp.arange(query_count, dtype=jnp.int32)
        key_pos = key_offset + jnp.arange(key_count, dtype=jnp.int32)
        allowed = key_pos[None, :] <= query_pos[:, None]
        score_matrix = jnp.where(allowed, score_matrix, neg_large)
        new_peak = jnp.maximum(row_peak, jnp.max(score_matrix, axis=-1))
        weights = jnp.where(allowed, jnp.exp(score_matrix - new_peak[..., None]), 0.0)
        fade_factor = jnp.exp(row_peak - new_peak)
        softmax_divisor = softmax_divisor * fade_factor + jnp.sum(weights, axis=-1)
        update = jnp.einsum(
            "bkgrs,bskd->bkgrd",
            weights.astype(jnp.bfloat16),
            value_block,
            preferred_element_type=jnp.float32,
        )
        accumulated = accumulated * fade_factor[..., None] + update
        return (new_peak, softmax_divisor, accumulated)

    def unchanged(previous):
        return previous

    return lax.cond(key_offset > query_offset + query_count - 1, unchanged, compute, carried)


def finish_rows(state_one):
    row_peak, softmax_divisor, accumulated = state_one
    normalised = accumulated / softmax_divisor[..., None]
    ordered = jnp.transpose(normalised, (0, 3, 1, 2, 4))
    return ordered.reshape(ordered.shape[0], ordered.shape[1], -1).astype(jnp.bfloat16)


def combine_carry(earlier, latter):
    return (earlier[0] * latter[0], latter[0] * earlier[1] + latter[1])


def shards(
    mixer_input,
    gate_input,
    step_input,
    state_proj,
    conv_weight,
    conv_bias,
    step_bias,
    decay_log,
    skip_gain,
    query_states,
    key_states,
    value_states,
    lengths,
):
    tap_count = conv_weight.shape[0]
    exchanged = (
        lax.all_to_all(mixer_input, "head", split_axis=2, concat_axis=1, tiled=True),
        lax.all_to_all(gate_input, "head", split_axis=2, concat_axis=1, tiled=True),
        lax.all_to_all(step_input, "head", split_axis=2, concat_axis=1, tiled=True),
        lax.all_to_all(query_states, "head", split_axis=2, concat_axis=1, tiled=True),
        lax.all_to_all(key_states, "head", split_axis=2, concat_axis=1, tiled=True),
        lax.all_to_all(value_states, "head", split_axis=2, concat_axis=1, tiled=True),
    )
    lead_local, gate_local, step_local, query_local, key_local, value_local = exchanged
    batch_size, row_count, channel_count = gate_local.shape
    channel_start = lax.axis_index("head") * channel_count
    weight_local = lax.dynamic_slice_in_dim(conv_weight, channel_start, channel_count, 1)
    bias_local = lax.dynamic_slice_in_dim(conv_bias, channel_start, channel_count, 0)
    tail_rows = lead_local[:, row_count - (tap_count - 1) :, :]
    before = passed_along(tail_rows, "ctx", 1)
    padded = jnp.concatenate([before, lead_local], axis=1)
    conv_out = conv_rows(padded, weight_local, bias_local, row_count)
    ctx_index = lax.axis_index("ctx")
    positions = ctx_index * row_count + jnp.arange(row_count, dtype=jnp.int32)
    live_rows = positions[None, :] < lengths[:, None]
    decay_rate = jnp.exp(decay_log)
    state_count = state_proj.shape[2] // 2
    conv_time = jnp.swapaxes(conv_out, 0, 1)
    step_time = jnp.swapaxes(step_local, 0, 1)
    proj_time = jnp.swapaxes(state_proj, 0, 1).astype(jnp.float32)
    readout_time = proj_time[:, :, state_count:]

    def advance(carry, inputs):
        state_now, elapsed_now = carry
        conv_row, step_row, proj_row = inputs
        step_row = jax.nn.softplus(step_row.astype(jnp.float32) + step_bias[None, :])
        elapsed_now = elapsed_now + step_row
        decay_now = jnp.exp(-step_row[:, None, :] * decay_rate[None])
        state_now = (
            decay_now * state_now
            + (step_row * conv_row.astype(jnp.float32))[:, None, :]
            * proj_row[:, :state_count, None]
        )
        return (
            (state_now, elapsed_now),
            (jnp.sum(proj_row[:, state_count:, None] * state_now, axis=1), elapsed_now),
        )

    start_state = jnp.zeros((batch_size, state_count, channel_count), jnp.float32)
    start_elapsed = jnp.zeros((batch_size, channel_count), jnp.float32)
    final_carry, scanned = lax.scan(
        advance, (start_state, start_elapsed), (conv_time, step_time, proj_time), unroll=8
    )
    final_state, total_elapsed = final_carry
    local_time, elapsed_time = scanned
    through = jnp.exp(-total_elapsed[:, None, :] * decay_rate[None])
    identity = (jnp.ones_like(through), jnp.zeros_like(final_state))
    prefix = carried_in((through, final_state), "ctx", combine_carry, identity)
    entering = prefix[1]
    carried = jnp.sum(
        readout_time[:, :, :, None]
        * jnp.exp(-elapsed_time[:, :, None, :] * decay_rate[None, None])
        * entering[None],
        axis=2,
    )
    mixed_time = (
        local_time + carried + skip_gain[None, None, :] * conv_time.astype(jnp.float32)
    ) * jax.nn.silu(jnp.swapaxes(gate_local, 0, 1).astype(jnp.float32))
    mixed_rows = jnp.swapaxes(mixed_time.astype(jnp.bfloat16), 0, 1)
    mixer_output = jnp.where(live_rows[:, :, None], mixed_rows, jnp.zeros((), jnp.bfloat16))
    kv_count = key_local.shape[2] // HD
    group_size = query_local.shape[2] // HD // kv_count
    query_five = query_local.reshape(batch_size, row_count, kv_count, group_size, HD)
    key_four = key_local.reshape(batch_size, row_count, kv_count, HD)
    value_four = value_local.reshape(batch_size, row_count, kv_count, HD)
    own_offset = ctx_index * row_count
    query_groups = [(query_five, own_offset)]
    logit_scale_factor = 1.0 / math.sqrt(HD)
    key_whole, value_whole = (
        lax.all_gather(key_four, "ctx", axis=1, tiled=True),
        lax.all_gather(value_four, "ctx", axis=1, tiled=True),
    )
    total_rows = key_whole.shape[1]
    chosen = block_width(total_rows)

    def one_block(block_index, current):
        key_block = lax.dynamic_slice_in_dim(key_whole, block_index * chosen, chosen, 1)
        value_block = lax.dynamic_slice_in_dim(value_whole, block_index * chosen, chosen, 1)
        key_offset = block_index * chosen
        return tuple(
            (
                attend_block(
                    state_one,
                    group[0],
                    group[1],
                    key_block,
                    value_block,
                    key_offset,
                    logit_scale_factor,
                )
                for state_one, group in zip(current, query_groups)
            )
        )

    initial = tuple((empty_state(group[0]) for group in query_groups))
    finished = lax.fori_loop(0, total_rows // chosen, one_block, initial)
    attended = finish_rows(finished[0])
    attention_output = jnp.where(live_rows[:, :, None], attended, jnp.zeros((), jnp.bfloat16))
    return (mixer_output, attention_output)


def solution(mesh):
    in_specs = (
        P(None, ("ctx", "head"), None),
        P(None, ("ctx", "head"), None),
        P(None, ("ctx", "head"), None),
        P(None, "ctx", None),
        P(),
        P(),
        P("head"),
        P(None, "head"),
        P("head"),
        P(None, ("ctx", "head"), None),
        P(None, ("ctx", "head"), None),
        P(None, ("ctx", "head"), None),
        P(),
    )
    out_specs = (P(None, "ctx", "head"), P(None, "ctx", "head"))
    return jax.shard_map(shards, mesh=mesh, in_specs=in_specs, out_specs=out_specs, check_vma=False)
```

profile of v0, /device:TPU:1, one launch (start us, length us, event | category | flops | bytes accessed | tf_op | source)
XLA Modules:
  0.0 620.2 jit_solution(5746733392723472344)
XLA Ops:
  9.0 9.3 %all_to_all.90 = bf16[4,2,4096]{2,1,0:T(2,128)(2,1)S(1)} all-to-all(bf16[4,2,4096]{2,1,0:T(2,128)(2,1)S(1)} %reshape.624), channel_id=1, replica_groups=mesh['ctx'=64,'head'=4] {'head'}, dimensions={0} | all-to-all | bytes 131072 | tf_op jit(solution)/shard_map/all_to_all | solution.py:132
  24.5 12.7 %copy.123 = bf16[2,16,16384]{1,0,2:T(2,128)(2,1)} copy(bf16[2,16,16384]{2,1,0:T(8,128)(2,1)S(1)} %copy-done.6) | data formatting | bytes 2097152 | tf_op args[0]
  37.3 10.9 %reshape.620 = bf16[4,2,65536]{2,1,0:T(2,128)(2,1)} reshape(bf16[16384,2,16]{2,1,0:T(2,128)(2,1)} %bitcast.310) | data formatting | bytes 2097152
  48.2 4.3 all-to-all-start.1
  52.5 12.7 %copy.120 = bf16[2,16,16384]{1,0,2:T(2,128)(2,1)} copy(bf16[2,16,16384]{2,1,0:T(8,128)(2,1)S(1)} %copy-done.7) | data formatting | bytes 2097152 | tf_op args[2]
  65.2 10.9 %reshape.622 = bf16[4,2,65536]{2,1,0:T(2,128)(2,1)} reshape(bf16[16384,2,16]{2,1,0:T(2,128)(2,1)} %bitcast.311) | data formatting | bytes 2097152
  76.1 4.4 all-to-all-start
  81.2 7.2 %reshape.621 = bf16[16384,2,16]{2,1,0:T(2,128)(2,1)} reshape(bf16[4,2,65536]{2,1,0:T(2,128)(2,1)S(1)} %all-to-all-done.1) | data formatting | bytes 2097152
  88.4 16.6 %copy.124 = bf16[2,16,4,4096]{3,1,2,0:T(8,128)(2,1)S(1)} copy(bf16[2,16,4,4096]{1,0,3,2:T(2,128)(2,1)} %bitcast.308) | data formatting | bytes 2097152 | tf_op jit(solution)/shard_map/all_to_all | solution.py:128
  105.7 6.2 %collective-permute-start = (bf16[2,3,4096]{2,1,0:T(4,128)(2,1)}, bf16[2,3,4096]{2,1,0:T(4,128)(2,1)}, u32[]{:S(2)}, u32[]{:S(2)}) collective-permute-start(bf16[2,3,4096]{2,1,0:T(4,128)(2,1)} %slice.220), channel_id=1, source_target_pairs={{0,4},{4,8},{8,12},{12,16},{16,20},{20,24},{24,28},{28,32},{32,36}... | collective-permute-start | bytes 147464 | tf_op jit(solution)/shard_map/ppermute | solution.py:14
  114.4 7.2 %reshape.623 = bf16[16384,2,16]{2,1,0:T(2,128)(2,1)} reshape(bf16[4,2,65536]{2,1,0:T(2,128)(2,1)S(1)} %all-to-all-done) | data formatting | bytes 2097152
  121.6 19.1 %copy.145 = bf16[2,16,4,4096]{3,2,1,0:T(4,128)(2,1)S(1)} copy(bf16[2,16,4,4096]{1,0,3,2:T(2,128)(2,1)} %bitcast.309) | data formatting | bytes 2097152 | tf_op jit(solution)/shard_map/all_to_all | solution.py:130
  144.5 58.9 %while.51 = (s32[]{:T(128)}, f32[2,16,4096]{2,1,0:T(8,128)S(1)}, f32[2,4096]{1,0:T(2,128)S(1)}, f32[8,8,2,4096]{3,1,0,2:T(8,128)}, f32[8,8,2,4096]{3,2,1,0:T(2,1...) while((s32[]{:T(128)}, f32[2,16,4096]{2,1,0:T(8,128)S(1)}, ...), condition=%wide.region_9.10_spmd.clone, body=%wide.region_0.9_spmd.clone.sunk | while | flops 10469385 | bytes 9039950 | solution.py:172
  204.9 6.7 %copy.135 = bf16[2,16,8192]{1,0,2:T(2,128)(2,1)} copy(bf16[2,16,8192]{2,1,0:T(8,128)(2,1)S(1)} %copy-done.9) | data formatting | bytes 1048576 | tf_op args[9]
  211.6 6.5 %reshape.626 = bf16[4,2,32768]{2,1,0:T(2,128)(2,1)} reshape(bf16[8192,2,16]{2,1,0:T(2,128)(2,1)} %bitcast.314) | data formatting | bytes 1048576
  218.2 4.5 all-to-all-start.4
  222.7 12.7 %copy.131 = bf16[2,16,16384]{1,0,2:T(2,128)(2,1)} copy(bf16[2,16,16384]{2,1,0:T(8,128)(2,1)S(1)} %copy-done.8) | data formatting | bytes 2097152 | tf_op args[1]
  235.3 10.9 %reshape.618 = bf16[4,2,65536]{2,1,0:T(2,128)(2,1)} reshape(bf16[16384,2,16]{2,1,0:T(2,128)(2,1)} %bitcast.312) | data formatting | bytes 2097152
  246.3 4.4 all-to-all-start.2
  250.8 4.1 reshape.627
  254.9 9.1 %copy.136 = bf16[2,16,4,2048]{3,1,2,0:T(8,128)(2,1)S(1)} copy(bf16[2,16,4,2048]{1,0,3,2:T(2,128)(2,1)} %bitcast.313) | data formatting | bytes 1048576 | tf_op jit(solution)/shard_map/all_to_all | solution.py:131
  266.1 7.1 %reshape.619 = bf16[16384,2,16]{2,1,0:T(2,128)(2,1)} reshape(bf16[4,2,65536]{2,1,0:T(2,128)(2,1)S(1)} %all-to-all-done.2) | data formatting | bytes 2097152
  273.2 18.8 %copy.132 = f32[2,16,4,4096]{3,1,2,0:T(8,128)} copy(bf16[2,16,4,4096]{1,0,3,2:T(2,128)(2,1)} %bitcast.307) | data formatting | bytes 3145728 | tf_op jit(solution)/shard_map/convert_element_type | solution.py:189
  292.1 4.9 neg.169
  296.9 5.0 copy.139
  301.9 4.7 copy.141
  306.7 6.5 %while.50 = (s32[]{:T(128)}, f32[2,2,8,64]{3,2,1,0:T(8,128)S(1)}, f32[2,2,8,64]{3,2,1,0:T(8,128)S(1)}, f32[2,2,8,64,128]{4,3,2,1,0:T(8,128)S(1)}, s32[]{:T(128)}...) while((s32[]{:T(128)}, f32[2,2,8,64]{3,2,1,0:T(8,128)S(1)}, ...), condition=%wide.region_18.19_spmd, body=%wide.region_13.18_spmd.sunk | while | flops 551064128 | bytes 16519977 | solution.py:227
  306.7 6.0 conditional.2
  315.0 34.7 %all-gather.6.cloned.1.call-done = f32[64,2,16,4096]{3,2,1,0:T(8,128)} async-done(((f32[1,2,16,4096]{3,2,1,0:T(8,128)}), f32[64,2,16,4096]{3,2,1,0:T(8,128)}) %all-gather.6.cloned.1.call-update) | async-done | bytes 33554448 | tf_op jit(solution)/shard_map/all_gather | solution.py:19
  349.7 142.1 %all-gather.12.cloned.1.call-done = f32[128,16,4096]{2,1,0:T(8,128)} async-done(((f32[2,16,4096]{2,1,0:T(8,128)}), f32[128,16,4096]{2,1,0:T(8,128)}) %all-gather.12.cloned.1.call-update) | async-done | bytes 33554448 | tf_op jit(solution)/shard_map/all_gather | solution.py:19
  491.9 105.7 %while.52 = (s32[]{:T(128)}, f32[2,16,4096]{2,1,0:T(8,128)S(1)}, s32[]{:T(128)}, f32[64,2,16,4096]{3,2,1,0:T(8,128)}, f32[64,2,16,4096]{3,2,1,0:T(8,128)}, /*index=5*/s32[]{:T(128)}, s32[]{:T(128)}) while((s32[]{:T(128)}, f32[2,16,4096]{2,1,0:T(8,128)S(1)}, s32[]{:T(128)}, f32[64,2,16,4096]{3,2,1,0:T(8,128)}, ...), condition=%wide.region_11.12_spmd.clone, body=%wide.region_10.11_spmd.clone.sunk | while | flops 524292 | bytes 2097253 | solution.py:28
  597.6 13.4 %multiply_reduce_fusion.8 = f32[64,2,4096]{2,1,0:T(2,128)S(1)} fusion(f32[2,16,4096]{2,1,0:T(8,128)S(1)} %get-tuple-element.472, f32[16,4096]{1,0:T(8,128)S(1)} %get-tuple-element.1256, f32[64,2,4096]{2,1,0:T(2,128)} %bitcast.327, f32[64,2,16]{2,1,0:T(2,128)S(1)} %copy.129), kind=kLoop, calls=%fused_computation.186 | loop fusion | flops 33030144 | bytes 4988928 | tf_op jit(solution)/shard_map/reduce_sum | solution.py:181
  (468 shorter events, 192.3 us)
Async XLA Ops:
  7.2 12.5 %copy-start.14 = (bf16[2,16,1024]{2,1,0:T(8,128)(2,1)S(1)}, bf16[2,16,1024]{2,1,0:T(8,128)(2,1)}, u32[]{:S(2)}) copy-start(bf16[2,16,1024]{2,1,0:T(8,128)(2,1)} %param.32) | copy-start | bytes 196612
  7.2 17.4 %copy-start.6 = (bf16[2,16,16384]{2,1,0:T(8,128)(2,1)S(1)}, bf16[2,16,16384]{2,1,0:T(8,128)(2,1)}, u32[]{:S(2)}) copy-start(bf16[2,16,16384]{2,1,0:T(8,128)(2,1)} %param.21) | copy-start | bytes 3145732
  7.2 289.7 %all-gather.8.cloned.1.call-start = ((), (), s32[]{:S(2)}) async-start(), calls=%async_computation.7 | async-start | bytes 4259840 | tf_op jit(solution)/shard_map/all_gather | solution.py:201
  21.2 27.0 %all-to-all-start.5 = ((bf16[4,2,4096]{2,1,0:T(2,128)(2,1)}), bf16[4,2,4096]{2,1,0:T(2,128)(2,1)S(1)}, u32[]{:S(2)}, u32[]{:S(2)}) async-start(bf16[4,2,4096]{2,1,0:T(2,128)(2,1)} %reshape.628), calls=%async_computation.5 | async-start | bytes 131072 | tf_op jit(solution)/shard_map/all_to_all | solution.py:133
  48.2 4.3 copy-start.7
  48.2 27.9 %all-to-all-start.1 = ((bf16[4,2,65536]{2,1,0:T(2,128)(2,1)}), bf16[4,2,65536]{2,1,0:T(2,128)(2,1)S(1)}, u32[]{:S(2)}, u32[]{:S(2)}) async-start(bf16[4,2,65536]{2,1,0:T(2,128)(2,1)} %reshape.620), calls=%async_computation.1 | async-start | bytes 2097152 | tf_op jit(solution)/shard_map/all_to_all | solution.py:128
  76.1 4.4 copy-start.15
  76.1 38.3 %all-to-all-start = ((bf16[4,2,65536]{2,1,0:T(2,128)(2,1)}), bf16[4,2,65536]{2,1,0:T(2,128)(2,1)S(1)}, u32[]{:S(2)}, u32[]{:S(2)}) async-start(bf16[4,2,65536]{2,1,0:T(2,128)(2,1)} %reshape.622), calls=%async_computation | async-start | bytes 2097152 | tf_op jit(solution)/shard_map/all_to_all | solution.py:130
  80.5 221.4 %all-gather.10.cloned.1.call-start = ((), (), s32[]{:S(2)}) async-start(), calls=%async_computation.8 | async-start | bytes 4259840 | tf_op jit(solution)/shard_map/all_gather | solution.py:202
  88.4 23.6 %copy-start.17 = (bf16[2,64,32]{1,2,0:T(8,128)(2,1)S(1)}, bf16[2,64,32]{1,2,0:T(8,128)(2,1)}, u32[]{:S(2)}) copy-start(bf16[2,64,32]{1,2,0:T(8,128)(2,1)} %param.24) | copy-start | bytes 24580
  88.4 23.6 %copy-start.10 = (f32[16,4096]{1,0:T(8,128)S(1)}, f32[16,4096]{1,0:T(8,128)}, u32[]{:S(2)}) copy-start(f32[16,4096]{1,0:T(8,128)} %param.28) | copy-start | bytes 786436
  105.0 16.6 %copy-start.3 = (bf16[2,16,4,4096]{3,1,2,0:T(8,128)(2,1)}, bf16[2,16,4,4096]{3,1,2,0:T(8,128)(2,1)S(1)}, u32[]{:S(2)}) copy-start(bf16[2,16,4,4096]{3,1,2,0:T(8,128)(2,1)S(1)} %copy.124) | copy-start | bytes 3145732
  105.7 35.7 %collective-permute-start = (bf16[2,3,4096]{2,1,0:T(4,128)(2,1)}, bf16[2,3,4096]{2,1,0:T(4,128)(2,1)}, u32[]{:S(2)}, u32[]{:S(2)}) collective-permute-start(bf16[2,3,4096]{2,1,0:T(4,128)(2,1)} %slice.220), channel_id=1, source_target_pairs={{0,4},{4,8},{8,12},{12,16},{16,20},{20,24},{24,28},{28,32},{32,36}... | collective-permute-start | bytes 147464 | tf_op jit(solution)/shard_map/ppermute | solution.py:14
  114.2 235.5 %all-gather.6.cloned.1.call-start = ((), (), s32[]{:S(2)}) async-start(), calls=%async_computation.6 | async-start | bytes 34078720 | tf_op jit(solution)/shard_map/all_gather | solution.py:19
  140.8 1.2 copy-start.4
  140.8 1.2 dynamic-slice-start
  140.8 1.2 copy-start.11
  140.8 1.2 copy-start.12
  140.8 1.2 copy-start.13
  140.8 3.7 copy-start.1
  203.4 1.0 copy-start
  203.4 1.5 copy-start.9
  204.4 287.5 %all-gather.12.cloned.1.call-start = ((), (), s32[]{:S(2)}) async-start(), calls=%async_computation.9 | async-start | bytes 34078720 | tf_op jit(solution)/shard_map/all_gather | solution.py:19
  211.6 11.0 %copy-start.8 = (bf16[2,16,16384]{2,1,0:T(8,128)(2,1)S(1)}, bf16[2,16,16384]{2,1,0:T(8,128)(2,1)}, u32[]{:S(2)}) copy-start(bf16[2,16,16384]{2,1,0:T(8,128)(2,1)} %param.22) | copy-start | bytes 3145732
  218.2 28.1 %all-to-all-start.4 = ((bf16[4,2,32768]{2,1,0:T(2,128)(2,1)}), bf16[4,2,32768]{2,1,0:T(2,128)(2,1)S(1)}, u32[]{:S(2)}, u32[]{:S(2)}) async-start(bf16[4,2,32768]{2,1,0:T(2,128)(2,1)} %reshape.626), calls=%async_computation.4 | async-start | bytes 1048576 | tf_op jit(solution)/shard_map/all_to_all | solution.py:131
  246.3 4.5 copy-start.18
  246.3 19.9 %all-to-all-start.2 = ((bf16[4,2,65536]{2,1,0:T(2,128)(2,1)}), bf16[4,2,65536]{2,1,0:T(2,128)(2,1)S(1)}, u32[]{:S(2)}, u32[]{:S(2)}) async-start(bf16[4,2,65536]{2,1,0:T(2,128)(2,1)} %reshape.618), calls=%async_computation.2 | async-start | bytes 2097152 | tf_op jit(solution)/shard_map/all_to_all | solution.py:129
  597.6 13.4 %copy-start.2 = (f32[2,16,4,4096]{3,1,2,0:T(8,128)S(1)}, f32[2,16,4,4096]{3,1,2,0:T(8,128)}, u32[]{:S(2)}) copy-start(f32[2,16,4,4096]{3,1,2,0:T(8,128)} %copy.132) | copy-start | bytes 6291460
  597.6 13.4 %copy-start.5 = (f32[8,8,2,4096]{3,1,0,2:T(8,128)S(1)}, f32[8,8,2,4096]{3,1,0,2:T(8,128)}, u32[]{:S(2)}) copy-start(f32[8,8,2,4096]{3,1,0,2:T(8,128)} %get-tuple-element.468) | copy-start | bytes 6291460
  597.6 13.4 %copy-start.16 = (f32[4096]{0:T(1024)S(1)}, f32[4096]{0:T(1024)}, u32[]{:S(2)}) copy-start(f32[4096]{0:T(1024)} %param.29) | copy-start | bytes 49156
Sparse Core Ops, SparseCore 0:
  19.8 81.7 all-gather.7
  114.3 81.8 all-gather.9
  204.5 145.1 all-gather.5
  352.3 139.4 all-gather.11
where the time goes:
time: 625 us; the launch traced here: 620 us
  local copies, waits for them, and re-layouts  220 us (35%)
  waiting for transfers between devices  179 us (29%)
  other arithmetic  163 us (26%)
  starting transfers between devices  27.3 us (4%)
  between operations  14.2 us (2%)
  blocking collectives  9.29 us (1%)
    all_gather x2, waiting for transfers between devices, carried_in(): pieces = jax.tree.map(lambda part: lax.all_gather(part, axis), value)  177 us
    unnamed x57, local copies, waits for them, and re-layouts  114 us
    select_n x63, other arithmetic, step(): jnp.where(position < mine, new, old)  104 us
    reduce_sum x24, other arithmetic, advance(): jnp.sum(proj_row[:, state_count:, None] * state_now, axis=1)  20.5 us
    all_to_all x2, local copies, waits for them, and re-layouts, shards(): lax.all_to_all(step_input, 'head', split_axis=2, concat_axis=1, tiled=True)  19.7 us
    convert_element_type x1, local copies, waits for them, and re-layouts, shards(): jnp.swapaxes(gate_local, 0, 1).astype(jnp.float32)  18.8 us
    all_to_all x1, local copies, waits for them, and re-layouts, shards(): lax.all_to_all(mixer_input, 'head', split_axis=2, concat_axis=1, tiled=True)  16.6 us
    reduce_sum x1, other arithmetic, shards(): jnp.sum(readout_time[:, :, :, None] * jnp.exp(-elapsed_time[:, :, None, :...  13.4 us
  transfers between devices with their start and end apart: 10, of which 3 were waited for; matrix products, arithmetic and copies ran while one was open for 42% of the time, Pallas kernels for 0%

commit v1 on v0

--- a/solution.py
+++ b/solution.py
@@ -6,6 +6,22 @@
 
 HD = 128
 neg_large = -1e30
+
+
+def swapped_with_each(x, axis, split, join):
+    ways, here = (lax.axis_size(axis), lax.axis_index(axis))
+    width = x.shape[split] // ways
+    lengths = list(x.shape)
+    lengths[split] = width
+    height = lengths[join]
+    lengths[join] = height * ways
+    full = jnp.zeros(lengths, x.dtype)
+    for mask in range(ways):
+        part = lax.dynamic_slice_in_dim(x, (here ^ mask) * width, width, axis=split)
+        if mask:
+            part = lax.ppermute(part, axis, [(d, d ^ mask) for d in range(ways)])
+        full = lax.dynamic_update_slice_in_dim(full, part, (here ^ mask) * height, axis=join)
+    return full
 
 
 def passed_along(block, axis, distance):
@@ -125,7 +141,7 @@
 ):
     tap_count = conv_weight.shape[0]
     exchanged = (
-        lax.all_to_all(mixer_input, "head", split_axis=2, concat_axis=1, tiled=True),
+        swapped_with_each(mixer_input, "head", 2, 1),
         lax.all_to_all(gate_input, "head", split_axis=2, concat_axis=1, tiled=True),
         lax.all_to_all(step_input, "head", split_axis=2, concat_axis=1, tiled=True),
         lax.all_to_all(query_states, "head", split_axis=2, concat_axis=1, tiled=True),

time: 625 us -> 598 us (0.957)
  local copies, waits for them, and re-layouts: 220 us -> 179 us
  waiting for transfers between devices: 179 us -> 197 us
    unnamed x57 -> x44, local copies, waits for them, and re-layouts: 114 us -> 86.7 us
    all_to_all x1 -> x0, local copies, waits for them, and re-layouts: 16.6 us -> none  [shards(): lax.all_to_all(mixer_input, 'head', split_axis=2, concat_axis=1, tiled=True)]
    all_to_all x1, waiting for transfers between devices: 0.01 us -> 9.32 us  [shards(): lax.all_to_all(step_input, 'head', split_axis=2, concat_axis=1, tiled=True)]
  transfers between devices with their start and end apart: 10 -> 12, of which waited for: 3 -> 5; matrix products, arithmetic and copies ran while one was open for 42% -> 37% of each run, Pallas kernels for 0% -> 0%
where the time goes in v1:
time: 598 us; the launch traced here: 594 us
  waiting for transfers between devices  197 us (33%)
  local copies, waits for them, and re-layouts  179 us (30%)
  other arithmetic  162 us (27%)
  starting transfers between devices  25.4 us (4%)
  between operations  14.2 us (2%)
  blocking collectives  9.29 us (2%)
    all_gather x2, waiting for transfers between devices, carried_in(): pieces = jax.tree.map(lambda part: lax.all_gather(part, axis), value)  181 us
    select_n x63, other arithmetic, step(): jnp.where(position < mine, new, old)  104 us
    unnamed x44, local copies, waits for them, and re-layouts  86.7 us
    all_to_all x2, local copies, waits for them, and re-layouts, shards(): lax.all_to_all(step_input, 'head', split_axis=2, concat_axis=1, tiled=True)  21.9 us
    reduce_sum x24, other arithmetic, advance(): jnp.sum(proj_row[:, state_count:, None] * state_now, axis=1)  20.5 us
    convert_element_type x1, local copies, waits for them, and re-layouts, shards(): jnp.swapaxes(gate_local, 0, 1).astype(jnp.float32)  18.8 us
    reduce_sum x1, other arithmetic, shards(): jnp.sum(readout_time[:, :, :, None] * jnp.exp(-elapsed_time[:, :, None, :...  13.4 us
    dynamic_update_slice x16, local copies, waits for them, and re-layouts, shards(): lax.scan(advance, (start_state, start_elapsed), (conv_time, step_time, pr...  12.8 us
  transfers between devices with their start and end apart: 12, of which 5 were waited for; matrix products, arithmetic and copies ran while one was open for 37% of the time, Pallas kernels for 0%

profile of v1, /device:TPU:1, one launch (start us, length us, event | category | flops | bytes accessed | tf_op | source)
XLA Modules:
  0.0 593.7 jit_solution(15792474687400682048)
XLA Ops:
  9.0 9.3 %all_to_all.72 = bf16[4,2,4096]{2,1,0:T(2,128)(2,1)S(1)} all-to-all(bf16[4,2,4096]{2,1,0:T(2,128)(2,1)S(1)} %reshape.622), channel_id=1, replica_groups=mesh['ctx'=64,'head'=4] {'head'}, dimensions={0} | all-to-all | bytes 131072 | tf_op jit(solution)/shard_map/all_to_all | solution.py:148
  26.1 3.3 all-to-all-start.4
  32.8 3.7 collective-permute-done.2
  36.6 5.5 collective-permute-start.3
  43.9 12.7 %copy.114 = bf16[2,16,16384]{1,0,2:T(2,128)(2,1)} copy(bf16[2,16,16384]{2,1,0:T(8,128)(2,1)S(1)} %copy-done.5) | data formatting | bytes 2097152 | tf_op args[2]
  56.6 10.9 %reshape.620 = bf16[4,2,65536]{2,1,0:T(2,128)(2,1)} reshape(bf16[16384,2,16]{2,1,0:T(2,128)(2,1)} %bitcast.303) | data formatting | bytes 2097152
  67.5 4.4 all-to-all-start
  74.2 2.5 multiply_convert_fusion
  76.8 9.3 %all-to-all-done = bf16[4,2,65536]{2,1,0:T(2,128)(2,1)} async-done(((bf16[4,2,65536]{2,1,0:T(2,128)(2,1)}), bf16[4,2,65536]{2,1,0:T(2,128)(2,1)}, u32[]{:S(2)}, u32[]{:S(2)}) %all-to-all-start) | async-done | bytes 1048608 | tf_op jit(solution)/shard_map/all_to_all | solution.py:146
  86.1 8.2 %reshape.621 = bf16[16384,2,16]{2,1,0:T(2,128)(2,1)} reshape(bf16[4,2,65536]{2,1,0:T(2,128)(2,1)} %all-to-all-done) | data formatting | bytes 2097152
  94.3 20.1 %copy.137 = bf16[2,16,4,4096]{3,2,1,0:T(4,128)(2,1)} copy(bf16[2,16,4,4096]{1,0,3,2:T(2,128)(2,1)} %bitcast.302) | data formatting | bytes 2097152 | tf_op jit(solution)/shard_map/all_to_all | solution.py:146
  116.2 59.0 %while.51 = (s32[]{:T(128)}, f32[2,16,4096]{2,1,0:T(8,128)S(1)}, f32[2,4096]{1,0:T(2,128)S(1)}, f32[8,8,2,4096]{3,1,0,2:T(8,128)}, f32[8,8,2,4096]{3,2,1,0:T(2,1...) while((s32[]{:T(128)}, f32[2,16,4096]{2,1,0:T(8,128)S(1)}, ...), condition=%wide.region_9.10_spmd.clone, body=%wide.region_0.9_spmd.clone.sunk | while | flops 10469385 | bytes 9039950 | solution.py:188
  176.8 6.7 %copy.127 = bf16[2,16,8192]{1,0,2:T(2,128)(2,1)} copy(bf16[2,16,8192]{2,1,0:T(8,128)(2,1)S(1)} %copy-done.8) | data formatting | bytes 1048576 | tf_op args[9]
  183.5 6.5 %reshape.624 = bf16[4,2,32768]{2,1,0:T(2,128)(2,1)} reshape(bf16[8192,2,16]{2,1,0:T(2,128)(2,1)} %bitcast.306) | data formatting | bytes 1048576
  190.0 3.5 all-to-all-start.3
  193.5 12.8 %copy.123 = bf16[2,16,16384]{1,0,2:T(2,128)(2,1)} copy(bf16[2,16,16384]{2,1,0:T(8,128)(2,1)S(1)} %copy-done.6) | data formatting | bytes 2097152 | tf_op args[1]
  206.3 11.0 %reshape.618 = bf16[4,2,65536]{2,1,0:T(2,128)(2,1)} reshape(bf16[16384,2,16]{2,1,0:T(2,128)(2,1)} %bitcast.304) | data formatting | bytes 2097152
  217.3 4.5 all-to-all-start.1
  222.0 4.1 reshape.625
  226.1 9.0 %copy.128 = bf16[2,16,4,2048]{3,1,2,0:T(8,128)(2,1)S(1)} copy(bf16[2,16,4,2048]{1,0,3,2:T(2,128)(2,1)} %bitcast.305) | data formatting | bytes 1048576 | tf_op jit(solution)/shard_map/all_to_all | solution.py:147
  239.7 7.1 %reshape.619 = bf16[16384,2,16]{2,1,0:T(2,128)(2,1)} reshape(bf16[4,2,65536]{2,1,0:T(2,128)(2,1)S(1)} %all-to-all-done.1) | data formatting | bytes 2097152
  246.8 18.8 %copy.124 = f32[2,16,4,4096]{3,1,2,0:T(8,128)} copy(bf16[2,16,4,4096]{1,0,3,2:T(2,128)(2,1)} %bitcast.301) | data formatting | bytes 3145728 | tf_op jit(solution)/shard_map/convert_element_type | solution.py:205
  265.5 4.9 copy.131
  270.5 5.0 copy.133
  275.6 6.5 %while.50 = (s32[]{:T(128)}, f32[2,2,8,64]{3,2,1,0:T(8,128)S(1)}, f32[2,2,8,64]{3,2,1,0:T(8,128)S(1)}, f32[2,2,8,64,128]{4,3,2,1,0:T(8,128)S(1)}, s32[]{:T(128)}...) while((s32[]{:T(128)}, f32[2,2,8,64]{3,2,1,0:T(8,128)S(1)}, ...), condition=%wide.region_18.19_spmd, body=%wide.region_13.18_spmd.sunk | while | flops 551064128 | bytes 16519977 | solution.py:243
  275.6 5.9 conditional.2
  279.0 2.6 fusion.6
  283.9 39.4 %all-gather.6.cloned.1.call-done = f32[64,2,16,4096]{3,2,1,0:T(8,128)} async-done(((f32[1,2,16,4096]{3,2,1,0:T(8,128)}), f32[64,2,16,4096]{3,2,1,0:T(8,128)}) %all-gather.6.cloned.1.call-update) | async-done | bytes 33554448 | tf_op jit(solution)/shard_map/all_gather | solution.py:35
  323.3 142.1 %all-gather.12.cloned.1.call-done = f32[128,16,4096]{2,1,0:T(8,128)} async-done(((f32[2,16,4096]{2,1,0:T(8,128)}), f32[128,16,4096]{2,1,0:T(8,128)}) %all-gather.12.cloned.1.call-update) | async-done | bytes 33554448 | tf_op jit(solution)/shard_map/all_gather | solution.py:35
  465.4 105.7 %while.52 = (s32[]{:T(128)}, f32[2,16,4096]{2,1,0:T(8,128)S(1)}, s32[]{:T(128)}, f32[64,2,16,4096]{3,2,1,0:T(8,128)}, f32[64,2,16,4096]{3,2,1,0:T(8,128)}, /*index=5*/s32[]{:T(128)}, s32[]{:T(128)}) while((s32[]{:T(128)}, f32[2,16,4096]{2,1,0:T(8,128)S(1)}, s32[]{:T(128)}, f32[64,2,16,4096]{3,2,1,0:T(8,128)}, ...), condition=%wide.region_11.12_spmd.clone, body=%wide.region_10.11_spmd.clone.sunk | while | flops 524292 | bytes 2097253 | solution.py:44
  571.1 13.4 %multiply_reduce_fusion.8 = f32[64,2,4096]{2,1,0:T(2,128)S(1)} fusion(f32[2,16,4096]{2,1,0:T(8,128)S(1)} %get-tuple-element.472, f32[16,4096]{1,0:T(8,128)S(1)} %get-tuple-element.1260, f32[64,2,4096]{2,1,0:T(2,128)} %bitcast.317, f32[64,2,16]{2,1,0:T(2,128)S(1)} %copy.121), kind=kLoop, calls=%fused_computation.186 | loop fusion | flops 33030144 | bytes 4988928 | tf_op jit(solution)/shard_map/reduce_sum | solution.py:197
  584.5 2.7 bitcast_select_fusion.1
  (463 shorter events, 192.8 us)
Async XLA Ops:
  7.2 12.6 %copy-start.7 = (bf16[2,16,16384]{2,1,0:T(8,128)(2,1)S(1)}, bf16[2,16,16384]{2,1,0:T(8,128)(2,1)}, u32[]{:S(2)}) copy-start(bf16[2,16,16384]{2,1,0:T(8,128)(2,1)} %param.21) | copy-start | bytes 3145732
  7.2 258.4 %all-gather.8.cloned.1.call-start = ((), (), s32[]{:S(2)}) async-start(), calls=%async_computation.6 | async-start | bytes 4259840 | tf_op jit(solution)/shard_map/all_gather | solution.py:217
  18.6 5.9 copy-start.9
  20.7 21.4 %copy-start.12 = (bf16[2,64,32]{1,2,0:T(8,128)(2,1)S(1)}, bf16[2,64,32]{1,2,0:T(8,128)(2,1)}, u32[]{:S(2)}) copy-start(bf16[2,64,32]{1,2,0:T(8,128)(2,1)} %param.24) | copy-start | bytes 24580
  20.7 23.2 %copy-start.5 = (bf16[2,16,16384]{2,1,0:T(8,128)(2,1)S(1)}, bf16[2,16,16384]{2,1,0:T(8,128)(2,1)}, u32[]{:S(2)}) copy-start(bf16[2,16,16384]{2,1,0:T(8,128)(2,1)} %param.23) | copy-start | bytes 3145732
  20.7 10.4 %collective-permute-start = (bf16[2,16,4096]{2,1,0:T(8,128)(2,1)}, bf16[2,16,4096]{2,1,0:T(8,128)(2,1)S(1)}, u32[]{:S(2)}, u32[]{:S(2)}) collective-permute-start(bf16[2,16,4096]{2,1,0:T(8,128)(2,1)} %get-tuple-element.807), channel_id=1, source_target_pairs={{0,1},{1,0},{2,3},{3,2},{4,5},{5,4},{6,7},{7,6},{8,9},{9,8},{10,11... | collective-permute-start | bytes 786440 | tf_op jit(solution)/shard_map/ppermute | solution.py:22
  21.0 11.8 %collective-permute-start.1 = (bf16[2,16,4096]{2,1,0:T(8,128)(2,1)}, bf16[2,16,4096]{2,1,0:T(8,128)(2,1)S(1)}, u32[]{:S(2)}, u32[]{:S(2)}) collective-permute-start(bf16[2,16,4096]{2,1,0:T(8,128)(2,1)} %get-tuple-element.809), channel_id=1, source_target_pairs={{0,2},{1,3},{2,0},{3,1},{4,6},{5,7},{6,4},{7,5},{8,10},{9,11},{10,... | collective-permute-start | bytes 786440 | tf_op jit(solution)/shard_map/ppermute | solution.py:22
  22.8 13.8 %collective-permute-start.2 = (bf16[2,16,4096]{2,1,0:T(8,128)(2,1)}, bf16[2,16,4096]{2,1,0:T(8,128)(2,1)S(1)}, u32[]{:S(2)}, u32[]{:S(2)}) collective-permute-start(bf16[2,16,4096]{2,1,0:T(8,128)(2,1)} %get-tuple-element.806), channel_id=1, source_target_pairs={{0,3},{1,2},{2,1},{3,0},{4,7},{5,6},{6,5},{7,4},{8,11},{9,10},{10,... | collective-permute-start | bytes 786440 | tf_op jit(solution)/shard_map/ppermute | solution.py:22
  26.1 41.5 %all-to-all-start.4 = ((bf16[4,2,4096]{2,1,0:T(2,128)(2,1)}), bf16[4,2,4096]{2,1,0:T(2,128)(2,1)S(1)}, u32[]{:S(2)}, u32[]{:S(2)}) async-start(bf16[4,2,4096]{2,1,0:T(2,128)(2,1)} %reshape.626), calls=%async_computation.4 | async-start | bytes 131072 | tf_op jit(solution)/shard_map/all_to_all | solution.py:149
  36.6 37.0 %collective-permute-start.3 = (bf16[2,3,4096]{2,1,0:T(4,128)(2,1)S(1)}, bf16[2,3,4096]{2,1,0:T(4,128)(2,1)S(1)}, u32[]{:S(2)}, u32[]{:S(2)}) collective-permute-start(bf16[2,3,4096]{2,1,0:T(4,128)(2,1)S(1)} %slice.220), channel_id=1, source_target_pairs={{0,4},{4,8},{8,12},{12,16},{16,20},{20,24},{24,28},{28,32},{32,36}... | collective-permute-start | bytes 147464 | tf_op jit(solution)/shard_map/ppermute | solution.py:30
  67.5 6.7 %dynamic-slice-start = ((f32[16384]{0:T(1024)}, s32[]{:T(128)}), f32[4096]{0:T(1024)S(1)}, s32[]{:S(2)}) async-start(f32[16384]{0:T(1024)} %param.26, s32[]{:T(128)} %select_n.162), calls=%async_computation.9 | async-start | bytes 33280 | tf_op jit(solution)/shard_map/dynamic_slice | solution.py:155
  67.5 18.6 %all-to-all-start = ((bf16[4,2,65536]{2,1,0:T(2,128)(2,1)}), bf16[4,2,65536]{2,1,0:T(2,128)(2,1)}, u32[]{:S(2)}, u32[]{:S(2)}) async-start(bf16[4,2,65536]{2,1,0:T(2,128)(2,1)} %reshape.620), calls=%async_computation | async-start | bytes 2097152 | tf_op jit(solution)/shard_map/all_to_all | solution.py:146
  71.9 198.6 %all-gather.10.cloned.1.call-start = ((), (), s32[]{:S(2)}) async-start(), calls=%async_computation.7 | async-start | bytes 4259840 | tf_op jit(solution)/shard_map/all_gather | solution.py:218
  73.4 249.9 %all-gather.6.cloned.1.call-start = ((), (), s32[]{:S(2)}) async-start(), calls=%async_computation.5 | async-start | bytes 34078720 | tf_op jit(solution)/shard_map/all_gather | solution.py:35
  73.6 0.6 copy-start.10
  114.4 1.8 copy-start.1
  175.2 1.0 copy-start
  175.2 1.5 copy-start.8
  176.2 289.2 %all-gather.12.cloned.1.call-start = ((), (), s32[]{:S(2)}) async-start(), calls=%async_computation.8 | async-start | bytes 34078720 | tf_op jit(solution)/shard_map/all_gather | solution.py:35
  183.5 10.0 %copy-start.6 = (bf16[2,16,16384]{2,1,0:T(8,128)(2,1)S(1)}, bf16[2,16,16384]{2,1,0:T(8,128)(2,1)}, u32[]{:S(2)}) copy-start(bf16[2,16,16384]{2,1,0:T(8,128)(2,1)} %param.22) | copy-start | bytes 3145732
  190.0 27.3 %all-to-all-start.3 = ((bf16[4,2,32768]{2,1,0:T(2,128)(2,1)}), bf16[4,2,32768]{2,1,0:T(2,128)(2,1)S(1)}, u32[]{:S(2)}, u32[]{:S(2)}) async-start(bf16[4,2,32768]{2,1,0:T(2,128)(2,1)} %reshape.624), calls=%async_computation.3 | async-start | bytes 1048576 | tf_op jit(solution)/shard_map/all_to_all | solution.py:147
  217.3 4.6 copy-start.13
  217.3 22.4 %all-to-all-start.1 = ((bf16[4,2,65536]{2,1,0:T(2,128)(2,1)}), bf16[4,2,65536]{2,1,0:T(2,128)(2,1)S(1)}, u32[]{:S(2)}, u32[]{:S(2)}) async-start(bf16[4,2,65536]{2,1,0:T(2,128)(2,1)} %reshape.618), calls=%async_computation.1 | async-start | bytes 2097152 | tf_op jit(solution)/shard_map/all_to_all | solution.py:145
  235.1 2.1 copy-start.3
  571.1 13.4 %copy-start.2 = (f32[2,16,4,4096]{3,1,2,0:T(8,128)S(1)}, f32[2,16,4,4096]{3,1,2,0:T(8,128)}, u32[]{:S(2)}) copy-start(f32[2,16,4,4096]{3,1,2,0:T(8,128)} %copy.124) | copy-start | bytes 6291460
  571.1 13.4 %copy-start.4 = (f32[8,8,2,4096]{3,1,0,2:T(8,128)S(1)}, f32[8,8,2,4096]{3,1,0,2:T(8,128)}, u32[]{:S(2)}) copy-start(f32[8,8,2,4096]{3,1,0,2:T(8,128)} %get-tuple-element.468) | copy-start | bytes 6291460
  571.1 13.4 %copy-start.11 = (f32[4096]{0:T(1024)S(1)}, f32[4096]{0:T(1024)}, u32[]{:S(2)}) copy-start(f32[4096]{0:T(1024)} %param.29) | copy-start | bytes 49156
Sparse Core Ops, SparseCore 0:
  19.8 81.7 all-gather.7
  104.4 76.1 all-gather.9
  183.4 139.8 all-gather.5
  325.9 139.4 all-gather.11
